TPU v7x, 256 devices: a whole 4x4x8 slice. The times are simulated.
256 devices in a mesh: grp: 4 (over z_hi), tile: 64 (over x, z_lo, y, core).
Axes of the slice: x: 4, y: 4, z: 8 (z_hi: 4, z_lo: 2; z = z_hi * 2 + z_lo), core: 2. Of those that a mesh axis runs over, the one named last changes fastest.
Arguments:
- ocean_state: bfloat16 [64, 4096, 512], P(None, 'tile', 'grp'), may hold values from -8 to 8
- sea_mask: int32 [4096, 512], P('tile', 'grp'), may hold values 0 or 1
- spectral_weights: float32 [2, 2, 32, 64, 64], replicated, may hold values from -0.75 to 0.75
- point_weights: bfloat16 [2, 64, 64], replicated, may hold values from -0.75 to 0.75
- point_bias: float32 [2, 64], replicated, may hold values from -4 to 4
- inner_weights: bfloat16 [2, 128, 64], replicated, may hold values from -0.75 to 0.75
- outer_weights: bfloat16 [2, 64, 128], replicated, may hold values from -0.5 to 0.5
- coarse_spectral: float32 [2, 32, 64, 64], replicated, may hold values from -0.75 to 0.75
- coarse_point: float32 [64, 64], replicated, may hold values from -0.75 to 0.75
- coarse_bias: float32 [64], replicated, may hold values from -2.5 to 2.5
Outputs:
- corrected: bfloat16 [64, 4096, 512], P(None, 'tile', 'grp')
Inputs may be any that keep to these rules, and one draw needn't show every extreme that they name: `sea_mask`: 1 marks a sea cell, 0 a land cell.
All inputs are finite; a program needn't handle non-finite values. No bound on the sum of `sea_mask` on one device may be relied on, other than what follows from the above.
Results may differ from a plain program's by a relative error of at most 0.0065.
Values may be sent and summed in bfloat16 or wider, within the bound.
A program may use at most 64 MiB of HBM per device.

v0:
```python
import math
import jax
import jax.numpy as jnp
from jax import lax
from jax.sharding import PartitionSpec as P

H = 64
R = 16
MX = 8
MY = 4
LAYERS = 2
PRECISE = lax.Precision.HIGHEST


def with_halo(x, sides, width):
    for axis, dim in sides:
        devices, length = (lax.axis_size(axis), x.shape[dim])
        up = [(i, (i + 1) % devices) for i in range(devices - 1)]
        down = [(j, i) for i, j in up]
        last = lax.slice_in_dim(x, length - width, length, axis=dim)
        first = lax.slice_in_dim(x, 0, width, axis=dim)
        before = lax.ppermute(last, axis, up)
        after = lax.ppermute(first, axis, down)
        x = jnp.concatenate([before, x, after], axis=dim)
    return x


def wave_numbers():
    order = jnp.arange(MX, dtype=jnp.int32)
    return jnp.where(order < MX // 2, order, order - MX)


def masked_table(positions, numbers, length):
    cycles = positions[:, None] * numbers[None, :] % length
    radians = cycles.astype(jnp.float32) * (2.0 * math.pi / length)
    inside = ((positions >= 0) & (positions < length)).astype(jnp.float32)[:, None]
    return (jnp.cos(radians) * inside, jnp.sin(radians) * inside)


def columns_transform(values, col_positions, col_length):
    channels, row_count, col_count = values.shape
    cos_cols, sin_cols = masked_table(col_positions, jnp.arange(MY, dtype=jnp.int32), col_length)
    lookup = jnp.concatenate([cos_cols, -sin_cols], axis=1)
    flattened = values.reshape(channels * row_count, col_count)
    return jnp.dot(
        flattened, lookup, precision=PRECISE, preferred_element_type=jnp.float32
    ).reshape(channels, row_count, 2 * MY)


def rows_transform(y_modes, row_positions, row_length):
    cos_rows, sin_rows = masked_table(row_positions, wave_numbers(), row_length)
    real_in = y_modes[:, :, :MY]
    imag_in = y_modes[:, :, MY:]
    coef_real = jnp.einsum("cxj,xi->cij", real_in, cos_rows, precision=PRECISE) + jnp.einsum(
        "cxj,xi->cij", imag_in, sin_rows, precision=PRECISE
    )
    coef_imag = jnp.einsum("cxj,xi->cij", imag_in, cos_rows, precision=PRECISE) - jnp.einsum(
        "cxj,xi->cij", real_in, sin_rows, precision=PRECISE
    )
    return jnp.stack([coef_real, coef_imag])


def forward(values, row_positions, col_positions, row_length, col_length):
    return rows_transform(
        columns_transform(values, col_positions, col_length), row_positions, row_length
    )


def mix_modes(coeffs, weights):
    channels = coeffs.shape[1]
    flattened = coeffs.reshape(2, channels, MX * MY)
    weight_real = weights[0]
    weight_imag = weights[1]
    mixed_real = jnp.einsum(
        "koc,ck->ok", weight_real, flattened[0], precision=PRECISE
    ) - jnp.einsum("koc,ck->ok", weight_imag, flattened[1], precision=PRECISE)
    mixed_imag = jnp.einsum(
        "koc,ck->ok", weight_real, flattened[1], precision=PRECISE
    ) + jnp.einsum("koc,ck->ok", weight_imag, flattened[0], precision=PRECISE)
    return (mixed_real, mixed_imag)


def synthesis(mixed_real, mixed_imag, row_positions, col_positions, row_length, col_length):
    channels = mixed_real.shape[0]
    grid_real = mixed_real.reshape(channels, MX, MY)
    grid_imag = mixed_imag.reshape(channels, MX, MY)
    cos_rows, sin_rows = masked_table(row_positions, wave_numbers(), row_length)
    part_real = jnp.einsum("cij,xi->cxj", grid_real, cos_rows, precision=PRECISE) - jnp.einsum(
        "cij,xi->cxj", grid_imag, sin_rows, precision=PRECISE
    )
    part_imag = jnp.einsum("cij,xi->cxj", grid_real, sin_rows, precision=PRECISE) + jnp.einsum(
        "cij,xi->cxj", grid_imag, cos_rows, precision=PRECISE
    )
    cos_cols, sin_cols = masked_table(col_positions, jnp.arange(MY, dtype=jnp.int32), col_length)
    weight = jnp.where(jnp.arange(MY) == 0, 1.0, 2.0).astype(jnp.float32)
    lookup = jnp.concatenate(
        [(cos_cols * weight[None, :]).T, -(sin_cols * weight[None, :]).T], axis=0
    )
    stacked = jnp.concatenate([part_real, part_imag], axis=2)
    row_count = stacked.shape[1]
    result = jnp.dot(stacked.reshape(channels * row_count, 2 * MY), lookup, precision=PRECISE)
    return result.reshape(channels, row_count, col_positions.shape[0])


def finish_layer(
    coeffs, interior, own_mask, ext_rows, ext_cols, spec, w_point, b_point, w_in, w_out
):
    channels, tile_rows, tile_cols = interior.shape
    cell_count = tile_rows * tile_cols
    mixed_real, mixed_imag = mix_modes(coeffs, spec)
    spectral = synthesis(
        mixed_real,
        mixed_imag,
        H + jnp.arange(tile_rows, dtype=jnp.int32),
        H + jnp.arange(tile_cols, dtype=jnp.int32),
        ext_rows,
        ext_cols,
    )
    pre_act = (
        spectral.reshape(channels, cell_count)
        + jnp.dot(
            w_point, interior.reshape(channels, cell_count), preferred_element_type=jnp.float32
        )
        + b_point[:, None]
    )
    activated = jax.nn.gelu(pre_act, approximate=True).astype(jnp.bfloat16)
    hidden = jax.nn.gelu(
        jnp.dot(w_in, activated, preferred_element_type=jnp.float32), approximate=True
    ).astype(jnp.bfloat16)
    result = jnp.dot(w_out, hidden, preferred_element_type=jnp.float32) * own_mask.reshape(
        1, cell_count
    ).astype(jnp.float32)
    return result.reshape(channels, tile_rows, tile_cols).astype(jnp.bfloat16)


def fine_step(interior, own_mask, spec, w_point, b_point, w_in, w_out):
    channels, tile_rows, tile_cols = interior.shape
    ext_rows = tile_rows + 2 * H
    ext_cols = tile_cols + 2 * H
    extended = with_halo(interior, (("grp", 2), ("tile", 1)), H)
    coeffs = forward(
        extended,
        jnp.arange(ext_rows, dtype=jnp.int32),
        jnp.arange(ext_cols, dtype=jnp.int32),
        ext_rows,
        ext_cols,
    )
    coeffs = coeffs / (ext_rows * ext_cols)
    return finish_layer(
        coeffs, interior, own_mask, ext_rows, ext_cols, spec, w_point, b_point, w_in, w_out
    )


def local(
    ocean_state,
    sea_mask,
    spectral_weights,
    point_weights,
    point_bias,
    inner_weights,
    outer_weights,
    coarse_spectral,
    coarse_point,
    coarse_bias,
):
    channels, tile_rows, tile_cols = ocean_state.shape
    current = jnp.where(sea_mask[None] > 0, ocean_state, jnp.zeros((), jnp.bfloat16))
    for layer_index in range(LAYERS):
        current = fine_step(
            current,
            sea_mask,
            spectral_weights[layer_index],
            point_weights[layer_index],
            point_bias[layer_index],
            inner_weights[layer_index],
            outer_weights[layer_index],
        )
    fine_values = current.astype(jnp.float32)
    block_rows = tile_rows // R
    block_cols = tile_cols // R
    coarse = fine_values.reshape(channels, block_rows, R, block_cols, R).sum(axis=(2, 4)) / (R * R)
    grid_rows = block_rows * lax.axis_size("tile")
    grid_cols = block_cols * lax.axis_size("grp")
    row_positions = lax.axis_index("tile") * block_rows + jnp.arange(block_rows, dtype=jnp.int32)
    col_positions = lax.axis_index("grp") * block_cols + jnp.arange(block_cols, dtype=jnp.int32)
    slab_piece = lax.all_gather(coarse, "tile", axis=1, tiled=True)
    piece_rows = slab_piece.shape[1]
    y_modes = columns_transform(slab_piece, col_positions, grid_cols)
    partial_sum = rows_transform(y_modes, jnp.arange(piece_rows, dtype=jnp.int32), grid_rows)
    coeffs = lax.psum(partial_sum, "grp")
    coeffs = coeffs / (grid_rows * grid_cols)
    mixed_real, mixed_imag = mix_modes(coeffs, coarse_spectral)
    spectral = synthesis(mixed_real, mixed_imag, row_positions, col_positions, grid_rows, grid_cols)
    local_term = jnp.dot(
        coarse_point, coarse.reshape(channels, block_rows * block_cols), precision=PRECISE
    )
    correction = (
        spectral + local_term.reshape(channels, block_rows, block_cols) + coarse_bias[:, None, None]
    )
    land_sea = sea_mask.astype(jnp.float32).reshape(1, block_rows, R, block_cols, R)
    corrected = (
        fine_values.reshape(channels, block_rows, R, block_cols, R)
        + correction[:, :, None, :, None] * land_sea
    )
    return corrected.reshape(channels, tile_rows, tile_cols).astype(jnp.bfloat16)


def solution(mesh):
    placed = (P(None, "tile", "grp"), P("tile", "grp"), P(), P(), P(), P(), P(), P(), P(), P())
    return jax.shard_map(
        local, mesh=mesh, in_specs=placed, out_specs=P(None, "tile", "grp"), check_vma=False
    )
```

profile of v0, /device:TPU:64, one launch (start us, length us, event | category | flops | bytes accessed | tf_op | source)
XLA Modules:
  0.0 372.4 jit_solution(2826999524209507329)
XLA Ops:
  2.6 6.4 %collective-permute-start = (bf16[64,64,64]{2,1,0:T(8,128)(2,1)S(1)}, bf16[64,64,64]{2,1,0:T(8,128)(2,1)S(1)}, u32[]{:S(2)}, u32[]{:S(2)}) collective-permute-start(bf16[64,64,64]{2,1,0:T(8,128)(2,1)S(1)} %get-tuple-element.7), channel_id=1, source_target_pairs={{0,64},{64,128},{128,192},{1,65},{65,129},{129,193},{2,66},{66,130... | collective-permute-start | bytes 1572872 | tf_op jit(solution)/shard_map/ppermute | solution.py:22
  10.9 42.9 %collective-permute-done = bf16[64,64,64]{2,1,0:T(8,128)(2,1)S(1)} collective-permute-done((bf16[64,64,64]{2,1,0:T(8,128)(2,1)S(1)}, bf16[64,64,64]{2,1,0:T(8,128)(2,1)S(1)}, u32[]{:S(2)}, u32[]{:S(2)}) %collective-permute-start) | collective-permute-done | bytes 524320 | tf_op jit(solution)/shard_map/ppermute | solution.py:22
  53.8 6.2 %collective-permute-done.1 = bf16[64,64,64]{2,1,0:T(8,128)(2,1)S(1)} collective-permute-done((bf16[64,64,64]{2,1,0:T(8,128)(2,1)S(1)}, bf16[64,64,64]{2,1,0:T(8,128)(2,1)S(1)}, u32[]{:S(2)}, u32[]{:S(2)}) %collective-permute-start.1) | collective-permute-done | bytes 524320 | tf_op jit(solution)/shard_map/ppermute | solution.py:23
  66.5 3.9 %collective-permute-done.3 = bf16[64,64,256]{2,1,0:T(8,128)(2,1)S(1)} collective-permute-done((bf16[64,64,256]{2,1,0:T(8,128)(2,1)S(1)}, bf16[64,64,256]{2,1,0:T(8,128)(2,1)S(1)}, u32[]{:S(2)}, u32[]{:S(2)}) %collective-permute-start.3) | collective-permute-done | bytes 2097184 | tf_op jit(solution)/shard_map/ppermute | solution.py:23
  70.4 5.1 %fusion.8 = f32[64,192,8]{1,2,0:T(8,128)S(1)} fusion(bf16[64,64,256]{2,1,0:T(8,128)(2,1)S(1)} %collective-permute-done.3, bf16[64,64,64]{2,1,0:T(8,128)(2,1)S(1)} %collective-permute-done.1, bf16[64,64,128]{2,1,0:T(8,128)(2,1)S(1)} %broadcast_select_fusion, bf16[64,64,64]{2,1,0:T(8,128)(2,1)S(1)} %collective-permute-done, ...), kind=kOutput, calls=%fused_computation.14 | convolution fusion | flops 333449216 | bytes 6692864 | tf_op jit(solution)/shard_map/dot_general | solution.py:45
  86.7 3.6 fusion.273
  91.9 3.1 fusion.51
  97.6 2.4 collective-permute-start.4
  100.0 4.4 %collective-permute-start.5 = (bf16[64,64,64]{2,1,0:T(8,128)(2,1)S(1)}, bf16[64,64,64]{2,1,0:T(8,128)(2,1)S(1)}, u32[]{:S(2)}, u32[]{:S(2)}) collective-permute-start(bf16[64,64,64]{2,1,0:T(8,128)(2,1)S(1)} %get-tuple-element.6), channel_id=1, source_target_pairs={{64,0},{128,64},{192,128},{65,1},{129,65},{193,129},{66,2},{130,66... | collective-permute-start | bytes 1572872 | tf_op jit(solution)/shard_map/ppermute | solution.py:23
  104.4 10.8 %collective-permute-done.4 = bf16[64,64,64]{2,1,0:T(8,128)(2,1)S(1)} collective-permute-done((bf16[64,64,64]{2,1,0:T(8,128)(2,1)S(1)}, bf16[64,64,64]{2,1,0:T(8,128)(2,1)S(1)}, u32[]{:S(2)}, u32[]{:S(2)}) %collective-permute-start.4) | collective-permute-done | bytes 524320 | tf_op jit(solution)/shard_map/ppermute | solution.py:22
  115.2 3.6 collective-permute-done.5
  120.1 43.0 %collective-permute-start.6 = (bf16[64,64,256]{2,1,0:T(8,128)(2,1)S(1)}, bf16[64,64,256]{2,1,0:T(8,128)(2,1)}, u32[]{:S(2)}, u32[]{:S(2)}) collective-permute-start(bf16[64,64,256]{2,1,0:T(8,128)(2,1)S(1)} %pad_maximum_fusion.1), channel_id=1, source_target_pairs={{0,1},{1,2},{2,3},{3,4},{4,5},{5,6},{6,7},{7,8},{8,9},{9,10},{10,1... | collective-permute-start | bytes 6291464 | tf_op jit(solution)/shard_map/ppermute | solution.py:22
  165.7 14.2 %collective-permute-done.7 = bf16[64,64,256]{2,1,0:T(8,128)(2,1)} collective-permute-done((bf16[64,64,256]{2,1,0:T(8,128)(2,1)S(1)}, bf16[64,64,256]{2,1,0:T(8,128)(2,1)}, u32[]{:S(2)}, u32[]{:S(2)}) %collective-permute-start.7) | collective-permute-done | bytes 2097184 | tf_op jit(solution)/shard_map/ppermute | solution.py:23
  179.9 7.6 %fusion.18 = f32[64,192,8]{1,2,0:T(8,128)S(1)} fusion(bf16[64,64,256]{2,1,0:T(8,128)(2,1)} %collective-permute-done.7, bf16[64,64,64]{2,1,0:T(8,128)(2,1)} %copy-done.6, bf16[64,64,128]{2,1,0:T(8,128)(2,1)S(1)} %bitcast.319, bf16[64,64,64]{2,1,0:T(8,128)(2,1)} %copy-done.5, bf16[64,64,256]{2,1,0:T(8,128)(2,1)} %collective-permute-done.6, ...), kind=kOutput, calls=%fused_computation.24 | convolution fusion | flops 333449216 | bytes 6692864 | tf_op jit(solution)/shard_map/dot_general | solution.py:45
  198.8 3.4 fusion.272
  204.0 3.6 fusion.59
  207.6 3.0 fusion.7
  210.7 2.8 copy.156
  213.4 2.6 reduce_sum.9
  216.1 105.2 %all_gather.3 = f32[64,256,8]{0,2,1:T(8,128)S(1)} all-gather(f32[64,4,8]{0,2,1:T(8,128)S(1)} %broadcast_multiply_fusion.1), channel_id=1, replica_groups=mesh['grp'=4,'tile'=64] {'tile'}, dimensions={1}, use_global_device_ids=true | all-gather | bytes 532480 | tf_op jit(solution)/shard_map/all_gather | solution.py:186
  321.3 7.4 %copy.116 = f32[64,256,8]{2,1,0:T(8,128)} copy(f32[64,256,8]{0,2,1:T(8,128)S(1)} %all_gather.3) | data formatting | bytes 1048576 | tf_op jit(solution)/shard_map/all_gather | solution.py:186
  328.7 9.8 %fusion.201 = f32[64,256,8]{1,2,0:T(8,128)S(1)} fusion(f32[64,256,8]{2,1,0:T(8,128)} %copy.116, f32[8,4]{0,1:T(4,128)S(1)} %get-tuple-element.28, f32[8,4]{0,1:T(4,128)S(1)} %get-tuple-element.27), kind=kOutput, calls=%fused_computation.257 | convolution fusion | flops 12582976 | bytes 1048832 | tf_op jit(solution)/shard_map/dot_general | solution.py:45
  340.6 18.2 %psum.7 = f32[2,64,8,4]{1,2,3,0:T(8,128)S(1)} all-reduce(f32[2,64,8,4]{1,2,3,0:T(8,128)S(1)} %pad_maximum_fusion.4), channel_id=1, replica_groups=mesh['grp'=4,'tile'=64] {'grp'}, use_global_device_ids=true, to_apply=%region_1.2 | all-reduce | flops 4096 | bytes 32768 | tf_op jit(solution)/shard_map/psum | solution.py:190
  369.6 2.3 copy.133
  (134 shorter events, 55.7 us)
Async XLA Ops:
  0.0 367.4 %copy-start = (f32[64,64]{1,0:T(8,128)S(1)}, f32[64,64]{1,0:T(8,128)}, u32[]{:S(2)}) copy-start(f32[64,64]{1,0:T(8,128)} %param.18) | copy-start | bytes 49156
  2.1 62.7 %copy-start.10 = (f32[2,64]{1,0:T(2,128)S(1)}, f32[2,64]{1,0:T(2,128)}, u32[]{:S(2)}) copy-start(f32[2,64]{1,0:T(2,128)} %param.14) | copy-start | bytes 1540
  2.1 62.8 %copy-start.9 = (s32[64,128]{1,0:T(8,128)S(1)}, s32[64,128]{1,0:T(8,128)}, u32[]{:S(2)}) copy-start(s32[64,128]{1,0:T(8,128)} %param.11) | copy-start | bytes 98308
  2.6 51.2 %collective-permute-start = (bf16[64,64,64]{2,1,0:T(8,128)(2,1)S(1)}, bf16[64,64,64]{2,1,0:T(8,128)(2,1)S(1)}, u32[]{:S(2)}, u32[]{:S(2)}) collective-permute-start(bf16[64,64,64]{2,1,0:T(8,128)(2,1)S(1)} %get-tuple-element.7), channel_id=1, source_target_pairs={{0,64},{64,128},{128,192},{1,65},{65,129},{129,193},{2,66},{66,130... | collective-permute-start | bytes 1572872 | tf_op jit(solution)/shard_map/ppermute | solution.py:22
  9.0 51.0 %collective-permute-start.1 = (bf16[64,64,64]{2,1,0:T(8,128)(2,1)S(1)}, bf16[64,64,64]{2,1,0:T(8,128)(2,1)S(1)}, u32[]{:S(2)}, u32[]{:S(2)}) collective-permute-start(bf16[64,64,64]{2,1,0:T(8,128)(2,1)S(1)} %get-tuple-element.8), channel_id=1, source_target_pairs={{64,0},{128,64},{192,128},{65,1},{129,65},{193,129},{66,2},{130,66... | collective-permute-start | bytes 1572872 | tf_op jit(solution)/shard_map/ppermute | solution.py:23
  61.2 5.2 %collective-permute-start.2 = (bf16[64,64,256]{2,1,0:T(8,128)(2,1)S(1)}, bf16[64,64,256]{2,1,0:T(8,128)(2,1)S(1)}, u32[]{:S(2)}, u32[]{:S(2)}) collective-permute-start(bf16[64,64,256]{2,1,0:T(8,128)(2,1)S(1)} %pad_maximum_fusion), channel_id=1, source_target_pairs={{0,1},{1,2},{2,3},{3,4},{4,5},{5,6},{6,7},{7,8},{8,9},{9,10},{10,1... | collective-permute-start | bytes 6291464 | tf_op jit(solution)/shard_map/ppermute | solution.py:22
  62.8 7.6 %collective-permute-start.3 = (bf16[64,64,256]{2,1,0:T(8,128)(2,1)S(1)}, bf16[64,64,256]{2,1,0:T(8,128)(2,1)S(1)}, u32[]{:S(2)}, u32[]{:S(2)}) collective-permute-start(bf16[64,64,256]{2,1,0:T(8,128)(2,1)S(1)} %pad_maximum_fusion), channel_id=1, source_target_pairs={{1,0},{2,1},{3,2},{4,3},{5,4},{6,5},{7,6},{8,7},{9,8},{10,9},{11,1... | collective-permute-start | bytes 6291464 | tf_op jit(solution)/shard_map/ppermute | solution.py:23
  70.4 7.2 %copy-start.2 = (f32[2,2,32,64,64]{4,3,2,1,0:T(8,128)S(1)}, f32[2,2,32,64,64]{4,3,2,1,0:T(8,128)}, u32[]{:S(2)}) copy-start(f32[2,2,32,64,64]{4,3,2,1,0:T(8,128)} %param.12) | copy-start | bytes 6291460
  85.5 6.4 %copy-start.12 = (bf16[2,64,64]{2,1,0:T(8,128)(2,1)S(1)}, bf16[2,64,64]{2,1,0:T(8,128)(2,1)}, u32[]{:S(2)}) copy-start(bf16[2,64,64]{2,1,0:T(8,128)(2,1)} %param.13) | copy-start | bytes 49156
  91.9 3.1 copy-start.13
  91.9 3.1 copy-start.14
  96.8 18.4 %copy-start.7 = (bf16[8192,64]{0,1:T(8,128)(2,1)}, bf16[8192,64]{0,1:T(8,128)(2,1)S(1)}, u32[]{:S(2)}) copy-start(bf16[8192,64]{0,1:T(8,128)(2,1)S(1)} %fusion.4) | copy-start | bytes 3145732
  97.6 17.6 %collective-permute-start.4 = (bf16[64,64,64]{2,1,0:T(8,128)(2,1)S(1)}, bf16[64,64,64]{2,1,0:T(8,128)(2,1)S(1)}, u32[]{:S(2)}, u32[]{:S(2)}) collective-permute-start(bf16[64,64,64]{2,1,0:T(8,128)(2,1)S(1)} %get-tuple-element.5), channel_id=1, source_target_pairs={{0,64},{64,128},{128,192},{1,65},{65,129},{129,193},{2,66},{66,130... | collective-permute-start | bytes 1572872 | tf_op jit(solution)/shard_map/ppermute | solution.py:22
  100.0 18.8 %collective-permute-start.5 = (bf16[64,64,64]{2,1,0:T(8,128)(2,1)S(1)}, bf16[64,64,64]{2,1,0:T(8,128)(2,1)S(1)}, u32[]{:S(2)}, u32[]{:S(2)}) collective-permute-start(bf16[64,64,64]{2,1,0:T(8,128)(2,1)S(1)} %get-tuple-element.6), channel_id=1, source_target_pairs={{64,0},{128,64},{192,128},{65,1},{129,65},{193,129},{66,2},{130,66... | collective-permute-start | bytes 1572872 | tf_op jit(solution)/shard_map/ppermute | solution.py:23
  115.2 49.4 %copy-start.5 = (bf16[64,64,64]{2,1,0:T(8,128)(2,1)}, bf16[64,64,64]{2,1,0:T(8,128)(2,1)S(1)}, u32[]{:S(2)}) copy-start(bf16[64,64,64]{2,1,0:T(8,128)(2,1)S(1)} %collective-permute-done.4) | copy-start | bytes 1572868
  118.8 45.8 %copy-start.6 = (bf16[64,64,64]{2,1,0:T(8,128)(2,1)}, bf16[64,64,64]{2,1,0:T(8,128)(2,1)S(1)}, u32[]{:S(2)}) copy-start(bf16[64,64,64]{2,1,0:T(8,128)(2,1)S(1)} %collective-permute-done.5) | copy-start | bytes 1572868
  120.1 45.6 %collective-permute-start.6 = (bf16[64,64,256]{2,1,0:T(8,128)(2,1)S(1)}, bf16[64,64,256]{2,1,0:T(8,128)(2,1)}, u32[]{:S(2)}, u32[]{:S(2)}) collective-permute-start(bf16[64,64,256]{2,1,0:T(8,128)(2,1)S(1)} %pad_maximum_fusion.1), channel_id=1, source_target_pairs={{0,1},{1,2},{2,3},{3,4},{4,5},{5,6},{6,7},{7,8},{8,9},{9,10},{10,1... | collective-permute-start | bytes 6291464 | tf_op jit(solution)/shard_map/ppermute | solution.py:22
  163.1 16.8 %collective-permute-start.7 = (bf16[64,64,256]{2,1,0:T(8,128)(2,1)S(1)}, bf16[64,64,256]{2,1,0:T(8,128)(2,1)}, u32[]{:S(2)}, u32[]{:S(2)}) collective-permute-start(bf16[64,64,256]{2,1,0:T(8,128)(2,1)S(1)} %pad_maximum_fusion.1), channel_id=1, source_target_pairs={{1,0},{2,1},{3,2},{4,3},{5,4},{6,5},{7,6},{8,7},{9,8},{10,9},{11,1... | collective-permute-start | bytes 6291464 | tf_op jit(solution)/shard_map/ppermute | solution.py:23
  164.8 24.8 %copy-start.3 = (f32[2,2,32,64,64]{4,3,2,1,0:T(8,128)S(1)}, f32[2,2,32,64,64]{4,3,2,1,0:T(8,128)}, u32[]{:S(2)}) copy-start(f32[2,2,32,64,64]{4,3,2,1,0:T(8,128)} %param.12) | copy-start | bytes 6291460
  197.6 6.4 %copy-start.8 = (bf16[8192,64]{0,1:T(8,128)(2,1)S(1)}, bf16[8192,64]{0,1:T(8,128)(2,1)}, u32[]{:S(2)}) copy-start(bf16[8192,64]{0,1:T(8,128)(2,1)} %copy-done.7) | copy-start | bytes 3145732
  328.7 30.2 %copy-start.4 = (f32[2,32,64,64]{3,2,1,0:T(8,128)S(1)}, f32[2,32,64,64]{3,2,1,0:T(8,128)}, u32[]{:S(2)}) copy-start(f32[2,32,64,64]{3,2,1,0:T(8,128)} %param.17) | copy-start | bytes 3145732
  338.5 28.9 %copy-start.11 = (f32[64]{0:T(128)S(1)}, f32[64]{0:T(128)}, u32[]{:S(2)}) copy-start(f32[64]{0:T(128)} %param.19) | copy-start | bytes 772
  360.6 7.5 %copy-start.1 = (f32[64,8192]{0,1:T(8,128)S(1)}, f32[64,8192]{0,1:T(8,128)}, u32[]{:S(2)}) copy-start(f32[64,8192]{0,1:T(8,128)} %copy.156) | copy-start | bytes 6291460
where the time goes:
time: 376 us; the launch traced here: 372 us
  blocking collectives  123 us (33%)
  waiting for transfers between devices  84 us (22%)
  matrix products  73.1 us (19%)
  starting transfers between devices  63 us (17%)
  local copies, waits for them, and re-layouts  18.4 us (5%)
  other arithmetic  9.35 us (2%)
    all_gather x1, blocking collectives, local(): slab_piece = lax.all_gather(coarse, 'tile', axis=1, tiled=True)  105 us
    ppermute x4, waiting for transfers between devices, with_halo(): before = lax.ppermute(last, axis, up)  56 us
    ppermute x4, starting transfers between devices, with_halo(): before = lax.ppermute(last, axis, up)  53.4 us
    ppermute x4, waiting for transfers between devices, with_halo(): after = lax.ppermute(first, axis, down)  28 us
    dot_general x3, matrix products, columns_transform(): jnp.dot(flattened, lookup, precision=PRECISE, preferred_element_type=jnp....  22.5 us
    psum x1, blocking collectives, local(): coeffs = lax.psum(partial_sum, 'grp')  18.2 us
    ppermute x4, starting transfers between devices, with_halo(): after = lax.ppermute(first, axis, down)  9.62 us
  transfers between devices with their start and end apart: 8, of which 8 were waited for; matrix products, arithmetic and copies ran while one was open for 0% of the time, Pallas kernels for 0%

commit v1 on v0

--- a/solution.py
+++ b/solution.py
@@ -183,7 +183,9 @@
     grid_cols = block_cols * lax.axis_size("grp")
     row_positions = lax.axis_index("tile") * block_rows + jnp.arange(block_rows, dtype=jnp.int32)
     col_positions = lax.axis_index("grp") * block_cols + jnp.arange(block_cols, dtype=jnp.int32)
-    slab_piece = lax.all_gather(coarse, "tile", axis=1, tiled=True)
+    slab_piece = jnp.concatenate(
+        lax.all_to_all(jnp.stack([coarse] * lax.axis_size("tile")), "tile", 0, 0), axis=1
+    )
     piece_rows = slab_piece.shape[1]
     y_modes = columns_transform(slab_piece, col_positions, grid_cols)
     partial_sum = rows_transform(y_modes, jnp.arange(piece_rows, dtype=jnp.int32), grid_rows)

time: 376 us -> 307 us (0.82)
  blocking collectives: 123 us -> 17.9 us
  starting transfers between devices: 63 us -> 95.8 us
  waiting for transfers between devices: 84 us -> 97.5 us
  matrix products: 73.1 us -> 62.7 us
    all_gather x1 -> x0, blocking collectives: 105 us -> none  [local(): slab_piece = lax.all_gather(coarse, 'tile', axis=1, tiled=True)]
    all_to_all x0 -> x1, starting transfers between devices: none -> 33.8 us  [local(): lax.all_to_all(jnp.stack([coarse] * lax.axis_size('tile')), 'tile', 0, 0)]
    all_to_all x0 -> x1, waiting for transfers between devices: none -> 12.2 us  [local(): lax.all_to_all(jnp.stack([coarse] * lax.axis_size('tile')), 'tile', 0, 0)]
    dot_general x3, matrix products: 22.5 us -> 11.7 us  [columns_transform(): jnp.dot(flattened, lookup, precision=PRECISE, preferred_element_type=jnp....]
    all_gather x1 -> x0, local copies, waits for them, and re-layouts: 7.39 us -> none  [local(): slab_piece = lax.all_gather(coarse, 'tile', axis=1, tiled=True)]
  transfers between devices with their start and end apart: 8 -> 9, of which waited for: 8 -> 9; matrix products, arithmetic and copies ran while one was open for 0% -> 0% of each run, Pallas kernels for 0% -> 0%
where the time goes in v1:
time: 307 us; the launch traced here: 302 us
  waiting for transfers between devices  97.5 us (32%)
  starting transfers between devices  95.8 us (31%)
  matrix products  62.7 us (20%)
  blocking collectives  17.9 us (6%)
  local copies, waits for them, and re-layouts  15.5 us (5%)
  other arithmetic  12.1 us (4%)
    ppermute x4, waiting for transfers between devices, with_halo(): before = lax.ppermute(last, axis, up)  57.3 us
    ppermute x4, starting transfers between devices, with_halo(): before = lax.ppermute(last, axis, up)  52.4 us
    all_to_all x1, starting transfers between devices, local(): lax.all_to_all(jnp.stack([coarse] * lax.axis_size('tile')), 'tile', 0, 0)  33.8 us
    ppermute x4, waiting for transfers between devices, with_halo(): after = lax.ppermute(first, axis, down)  28 us
    psum x1, blocking collectives, local(): coeffs = lax.psum(partial_sum, 'grp')  17.9 us
    all_to_all x1, waiting for transfers between devices, local(): lax.all_to_all(jnp.stack([coarse] * lax.axis_size('tile')), 'tile', 0, 0)  12.2 us
    dot_general x3, matrix products, columns_transform(): jnp.dot(flattened, lookup, precision=PRECISE, preferred_element_type=jnp....  11.7 us
    ppermute x4, starting transfers between devices, with_halo(): after = lax.ppermute(first, axis, down)  9.64 us
  transfers between devices with their start and end apart: 9, of which 9 were waited for; matrix products, arithmetic and copies ran while one was open for 0% of the time, Pallas kernels for 0%

profile of v1, /device:TPU:64, one launch (start us, length us, event | category | flops | bytes accessed | tf_op | source)
XLA Modules:
  0.0 302.4 jit_solution(5410705029497908210)
XLA Ops:
  2.6 6.4 %collective-permute-start = (bf16[64,64,64]{2,1,0:T(8,128)(2,1)S(1)}, bf16[64,64,64]{2,1,0:T(8,128)(2,1)S(1)}, u32[]{:S(2)}, u32[]{:S(2)}) collective-permute-start(bf16[64,64,64]{2,1,0:T(8,128)(2,1)S(1)} %get-tuple-element.7), channel_id=1, source_target_pairs={{0,64},{64,128},{128,192},{1,65},{65,129},{129,193},{2,66},{66,130... | collective-permute-start | bytes 1572872 | tf_op jit(solution)/shard_map/ppermute | solution.py:22
  10.9 42.9 %collective-permute-done = bf16[64,64,64]{2,1,0:T(8,128)(2,1)S(1)} collective-permute-done((bf16[64,64,64]{2,1,0:T(8,128)(2,1)S(1)}, bf16[64,64,64]{2,1,0:T(8,128)(2,1)S(1)}, u32[]{:S(2)}, u32[]{:S(2)}) %collective-permute-start) | collective-permute-done | bytes 524320 | tf_op jit(solution)/shard_map/ppermute | solution.py:22
  53.8 6.2 %collective-permute-done.1 = bf16[64,64,64]{2,1,0:T(8,128)(2,1)S(1)} collective-permute-done((bf16[64,64,64]{2,1,0:T(8,128)(2,1)S(1)}, bf16[64,64,64]{2,1,0:T(8,128)(2,1)S(1)}, u32[]{:S(2)}, u32[]{:S(2)}) %collective-permute-start.1) | collective-permute-done | bytes 524320 | tf_op jit(solution)/shard_map/ppermute | solution.py:23
  66.5 3.9 %collective-permute-done.3 = bf16[64,64,256]{2,1,0:T(8,128)(2,1)S(1)} collective-permute-done((bf16[64,64,256]{2,1,0:T(8,128)(2,1)S(1)}, bf16[64,64,256]{2,1,0:T(8,128)(2,1)S(1)}, u32[]{:S(2)}, u32[]{:S(2)}) %collective-permute-start.3) | collective-permute-done | bytes 2097184 | tf_op jit(solution)/shard_map/ppermute | solution.py:23
  70.4 5.1 %fusion.8 = f32[64,192,8]{1,2,0:T(8,128)S(1)} fusion(bf16[64,64,256]{2,1,0:T(8,128)(2,1)S(1)} %collective-permute-done.3, bf16[64,64,64]{2,1,0:T(8,128)(2,1)S(1)} %collective-permute-done.1, bf16[64,64,128]{2,1,0:T(8,128)(2,1)S(1)} %broadcast_select_fusion, bf16[64,64,64]{2,1,0:T(8,128)(2,1)S(1)} %collective-permute-done, ...), kind=kOutput, calls=%fused_computation.14 | convolution fusion | flops 333449216 | bytes 6692864 | tf_op jit(solution)/shard_map/dot_general | solution.py:45
  86.7 3.6 %fusion.277 = f32[4096,128]{1,0:T(8,128)S(1)} fusion(f32[4096,8]{0,1:T(8,128)S(1)} %reshape.178, f32[4,128]{1,0:T(4,128)S(1)} %get-tuple-element.26, f32[4,128]{1,0:T(4,128)S(1)} %get-tuple-element.25), kind=kOutput, calls=%fused_computation.330 | convolution fusion | flops 50332672 | bytes 2232320 | tf_op jit(solution)/shard_map/dot_general | solution.py:101
  91.9 3.1 %fusion.51 = bf16[64,8192]{1,0:T(8,128)(2,1)S(1)} fusion(f32[64,8192]{1,0:T(8,128)} %reshape_reshape.7, bf16[8,8,64,128]{3,2,1,0:T(8,128)(2,1)S(1)} %bitcast.320, f32[64]{0:T(128)S(1)} %get-tuple-element.30, bf16[2,64,64]{2,1,0:T(8,128)(2,1)S(1)} %copy-done.8), kind=kOutput, calls=%fused_computation.62 | convolution fusion | flops 72876032 | bytes 4211200 | tf_op jit(solution)/shard_map/dot_general | solution.py:121
  97.5 2.4 collective-permute-start.4
  100.0 4.4 %collective-permute-start.5 = (bf16[64,64,64]{2,1,0:T(8,128)(2,1)S(1)}, bf16[64,64,64]{2,1,0:T(8,128)(2,1)S(1)}, u32[]{:S(2)}, u32[]{:S(2)}) collective-permute-start(bf16[64,64,64]{2,1,0:T(8,128)(2,1)S(1)} %get-tuple-element.6), channel_id=1, source_target_pairs={{64,0},{128,64},{192,128},{65,1},{129,65},{193,129},{66,2},{130,66... | collective-permute-start | bytes 1572872 | tf_op jit(solution)/shard_map/ppermute | solution.py:23
  104.4 10.8 %collective-permute-done.4 = bf16[64,64,64]{2,1,0:T(8,128)(2,1)S(1)} collective-permute-done((bf16[64,64,64]{2,1,0:T(8,128)(2,1)S(1)}, bf16[64,64,64]{2,1,0:T(8,128)(2,1)S(1)}, u32[]{:S(2)}, u32[]{:S(2)}) %collective-permute-start.4) | collective-permute-done | bytes 524320 | tf_op jit(solution)/shard_map/ppermute | solution.py:22
  115.1 3.6 %collective-permute-done.5 = bf16[64,64,64]{2,1,0:T(8,128)(2,1)S(1)} collective-permute-done((bf16[64,64,64]{2,1,0:T(8,128)(2,1)S(1)}, bf16[64,64,64]{2,1,0:T(8,128)(2,1)S(1)}, u32[]{:S(2)}, u32[]{:S(2)}) %collective-permute-start.5) | collective-permute-done | bytes 524320 | tf_op jit(solution)/shard_map/ppermute | solution.py:23
  120.1 42.0 %collective-permute-start.6 = (bf16[64,64,256]{2,1,0:T(8,128)(2,1)S(1)}, bf16[64,64,256]{2,1,0:T(8,128)(2,1)S(1)}, u32[]{:S(2)}, u32[]{:S(2)}) collective-permute-start(bf16[64,64,256]{2,1,0:T(8,128)(2,1)S(1)} %pad_maximum_fusion.1), channel_id=1, source_target_pairs={{0,1},{1,2},{2,3},{3,4},{4,5},{5,6},{6,7},{7,8},{8,9},{9,10},{10,1... | collective-permute-start | bytes 6291464 | tf_op jit(solution)/shard_map/ppermute | solution.py:22
  165.7 14.2 %collective-permute-done.7 = bf16[64,64,256]{2,1,0:T(8,128)(2,1)S(1)} collective-permute-done((bf16[64,64,256]{2,1,0:T(8,128)(2,1)S(1)}, bf16[64,64,256]{2,1,0:T(8,128)(2,1)S(1)}, u32[]{:S(2)}, u32[]{:S(2)}) %collective-permute-start.7) | collective-permute-done | bytes 2097184 | tf_op jit(solution)/shard_map/ppermute | solution.py:23
  180.0 5.0 %fusion.18 = f32[64,192,8]{1,2,0:T(8,128)S(1)} fusion(bf16[64,64,256]{2,1,0:T(8,128)(2,1)S(1)} %collective-permute-done.7, bf16[64,64,64]{2,1,0:T(8,128)(2,1)S(1)} %collective-permute-done.5, bf16[64,64,128]{2,1,0:T(8,128)(2,1)S(1)} %bitcast.323, bf16[64,64,64]{2,1,0:T(8,128)(2,1)S(1)} %collective-permute-done.4, ...), kind=kOutput, calls=%fused_computation.24 | convolution fusion | flops 333449216 | bytes 6692864 | tf_op jit(solution)/shard_map/dot_general | solution.py:45
  196.3 3.8 %fusion.276 = f32[4096,128]{1,0:T(8,128)S(1)} fusion(f32[4096,8]{0,1:T(8,128)S(1)} %reshape.182, f32[4,128]{1,0:T(4,128)S(1)} %get-tuple-element.26, f32[4,128]{1,0:T(4,128)S(1)} %get-tuple-element.25), kind=kOutput, calls=%fused_computation.329 | convolution fusion | flops 50332672 | bytes 2232320 | tf_op jit(solution)/shard_map/dot_general | solution.py:101
  201.6 3.6 %fusion.59 = bf16[64,8192]{1,0:T(8,128)(2,1)} fusion(f32[64,8192]{1,0:T(8,128)} %reshape_reshape.8, bf16[8192,64]{0,1:T(8,128)(2,1)S(1)} %fusion.4, f32[64]{0:T(128)S(1)} %get-tuple-element.29, bf16[2,64,64]{2,1,0:T(8,128)(2,1)S(1)} %copy-done.8), kind=kOutput, calls=%fused_computation.70 | convolution fusion | flops 72876032 | bytes 4211200 | tf_op jit(solution)/shard_map/dot_general | solution.py:121
  205.2 3.0 %fusion.7 = f32[64,8192]{1,0:T(8,128)S(1)} fusion(bf16[64,8192]{1,0:T(8,128)(2,1)} %fusion.59, f32[8192]{0:T(1024)S(1)} %get-tuple-element.16, bf16[2,64,128]{2,1,0:T(8,128)(2,1)S(1)} %copy-done.9, bf16[2,128,64]{1,2,0:T(8,128)(2,1)S(1)} %copy-done.10), kind=kOutput, calls=%fused_computation.13 | convolution fusion | flops 279445504 | bytes 3211264 | tf_op jit(solution)/shard_map/dot_general | solution.py:130
  208.3 2.7 copy.80
  211.0 2.6 reduce_sum.9
  215.2 33.8 %all-to-all-start = ((f32[64,1,2048]{2,1,0:T(1,128)}), f32[64,1,2048]{2,1,0:T(1,128)S(1)}, u32[]{:S(2)}, u32[]{:S(2)}) async-start(f32[64,1,2048]{2,1,0:T(1,128)} %reshape.218), calls=%async_computation | async-start | bytes 1048576 | tf_op jit(solution)/shard_map/all_to_all | solution.py:187
  249.2 12.2 %all-to-all-done = f32[64,1,2048]{2,1,0:T(1,128)S(1)} async-done(((f32[64,1,2048]{2,1,0:T(1,128)}), f32[64,1,2048]{2,1,0:T(1,128)S(1)}, u32[]{:S(2)}, u32[]{:S(2)}) %all-to-all-start) | async-done | bytes 524320 | tf_op jit(solution)/shard_map/all_to_all | solution.py:187
  262.0 2.8 reduce
  271.2 17.9 %psum.7 = f32[2,64,8,4]{1,2,3,0:T(8,128)S(1)} all-reduce(f32[2,64,8,4]{1,2,3,0:T(8,128)S(1)} %pad_maximum_fusion.4), channel_id=1, replica_groups=mesh['grp'=4,'tile'=64] {'grp'}, use_global_device_ids=true, to_apply=%region_1.2 | all-reduce | flops 4096 | bytes 32768 | tf_op jit(solution)/shard_map/psum | solution.py:192
  299.8 2.3 copy.55
  (132 shorter events, 63.1 us)
Async XLA Ops:
  0.0 297.6 %copy-start = (f32[64,64]{1,0:T(8,128)S(1)}, f32[64,64]{1,0:T(8,128)}, u32[]{:S(2)}) copy-start(f32[64,64]{1,0:T(8,128)} %param.18) | copy-start | bytes 49156
  2.1 62.7 %copy-start.6 = (f32[2,64]{1,0:T(2,128)S(1)}, f32[2,64]{1,0:T(2,128)}, u32[]{:S(2)}) copy-start(f32[2,64]{1,0:T(2,128)} %param.14) | copy-start | bytes 1540
  2.1 62.8 %copy-start.5 = (s32[64,128]{1,0:T(8,128)S(1)}, s32[64,128]{1,0:T(8,128)}, u32[]{:S(2)}) copy-start(s32[64,128]{1,0:T(8,128)} %param.11) | copy-start | bytes 98308
  2.6 51.2 %collective-permute-start = (bf16[64,64,64]{2,1,0:T(8,128)(2,1)S(1)}, bf16[64,64,64]{2,1,0:T(8,128)(2,1)S(1)}, u32[]{:S(2)}, u32[]{:S(2)}) collective-permute-start(bf16[64,64,64]{2,1,0:T(8,128)(2,1)S(1)} %get-tuple-element.7), channel_id=1, source_target_pairs={{0,64},{64,128},{128,192},{1,65},{65,129},{129,193},{2,66},{66,130... | collective-permute-start | bytes 1572872 | tf_op jit(solution)/shard_map/ppermute | solution.py:22
  9.0 51.0 %collective-permute-start.1 = (bf16[64,64,64]{2,1,0:T(8,128)(2,1)S(1)}, bf16[64,64,64]{2,1,0:T(8,128)(2,1)S(1)}, u32[]{:S(2)}, u32[]{:S(2)}) collective-permute-start(bf16[64,64,64]{2,1,0:T(8,128)(2,1)S(1)} %get-tuple-element.8), channel_id=1, source_target_pairs={{64,0},{128,64},{192,128},{65,1},{129,65},{193,129},{66,2},{130,66... | collective-permute-start | bytes 1572872 | tf_op jit(solution)/shard_map/ppermute | solution.py:23
  61.2 5.2 %collective-permute-start.2 = (bf16[64,64,256]{2,1,0:T(8,128)(2,1)S(1)}, bf16[64,64,256]{2,1,0:T(8,128)(2,1)S(1)}, u32[]{:S(2)}, u32[]{:S(2)}) collective-permute-start(bf16[64,64,256]{2,1,0:T(8,128)(2,1)S(1)} %pad_maximum_fusion), channel_id=1, source_target_pairs={{0,1},{1,2},{2,3},{3,4},{4,5},{5,6},{6,7},{7,8},{8,9},{9,10},{10,1... | collective-permute-start | bytes 6291464 | tf_op jit(solution)/shard_map/ppermute | solution.py:22
  62.8 7.6 %collective-permute-start.3 = (bf16[64,64,256]{2,1,0:T(8,128)(2,1)S(1)}, bf16[64,64,256]{2,1,0:T(8,128)(2,1)S(1)}, u32[]{:S(2)}, u32[]{:S(2)}) collective-permute-start(bf16[64,64,256]{2,1,0:T(8,128)(2,1)S(1)} %pad_maximum_fusion), channel_id=1, source_target_pairs={{1,0},{2,1},{3,2},{4,3},{5,4},{6,5},{7,6},{8,7},{9,8},{10,9},{11,1... | collective-permute-start | bytes 6291464 | tf_op jit(solution)/shard_map/ppermute | solution.py:23
  70.4 7.2 %copy-start.2 = (f32[2,2,32,64,64]{4,3,2,1,0:T(8,128)S(1)}, f32[2,2,32,64,64]{4,3,2,1,0:T(8,128)}, u32[]{:S(2)}) copy-start(f32[2,2,32,64,64]{4,3,2,1,0:T(8,128)} %param.12) | copy-start | bytes 6291460
  85.5 6.3 %copy-start.8 = (bf16[2,64,64]{2,1,0:T(8,128)(2,1)S(1)}, bf16[2,64,64]{2,1,0:T(8,128)(2,1)}, u32[]{:S(2)}) copy-start(bf16[2,64,64]{2,1,0:T(8,128)(2,1)} %param.13) | copy-start | bytes 49156
  91.9 3.1 %copy-start.9 = (bf16[2,64,128]{2,1,0:T(8,128)(2,1)S(1)}, bf16[2,64,128]{2,1,0:T(8,128)(2,1)}, u32[]{:S(2)}) copy-start(bf16[2,64,128]{2,1,0:T(8,128)(2,1)} %param.16) | copy-start | bytes 98308
  91.9 3.1 %copy-start.10 = (bf16[2,128,64]{1,2,0:T(8,128)(2,1)S(1)}, bf16[2,128,64]{1,2,0:T(8,128)(2,1)}, u32[]{:S(2)}) copy-start(bf16[2,128,64]{1,2,0:T(8,128)(2,1)} %param.15) | copy-start | bytes 98308
  97.5 17.6 %collective-permute-start.4 = (bf16[64,64,64]{2,1,0:T(8,128)(2,1)S(1)}, bf16[64,64,64]{2,1,0:T(8,128)(2,1)S(1)}, u32[]{:S(2)}, u32[]{:S(2)}) collective-permute-start(bf16[64,64,64]{2,1,0:T(8,128)(2,1)S(1)} %get-tuple-element.5), channel_id=1, source_target_pairs={{0,64},{64,128},{128,192},{1,65},{65,129},{129,193},{2,66},{66,130... | collective-permute-start | bytes 1572872 | tf_op jit(solution)/shard_map/ppermute | solution.py:22
  100.0 18.8 %collective-permute-start.5 = (bf16[64,64,64]{2,1,0:T(8,128)(2,1)S(1)}, bf16[64,64,64]{2,1,0:T(8,128)(2,1)S(1)}, u32[]{:S(2)}, u32[]{:S(2)}) collective-permute-start(bf16[64,64,64]{2,1,0:T(8,128)(2,1)S(1)} %get-tuple-element.6), channel_id=1, source_target_pairs={{64,0},{128,64},{192,128},{65,1},{129,65},{193,129},{66,2},{130,66... | collective-permute-start | bytes 1572872 | tf_op jit(solution)/shard_map/ppermute | solution.py:23
  120.0 67.1 %copy-start.3 = (f32[2,2,32,64,64]{4,3,2,1,0:T(8,128)S(1)}, f32[2,2,32,64,64]{4,3,2,1,0:T(8,128)}, u32[]{:S(2)}) copy-start(f32[2,2,32,64,64]{4,3,2,1,0:T(8,128)} %param.12) | copy-start | bytes 6291460
  120.1 45.7 %collective-permute-start.6 = (bf16[64,64,256]{2,1,0:T(8,128)(2,1)S(1)}, bf16[64,64,256]{2,1,0:T(8,128)(2,1)S(1)}, u32[]{:S(2)}, u32[]{:S(2)}) collective-permute-start(bf16[64,64,256]{2,1,0:T(8,128)(2,1)S(1)} %pad_maximum_fusion.1), channel_id=1, source_target_pairs={{0,1},{1,2},{2,3},{3,4},{4,5},{5,6},{6,7},{7,8},{8,9},{9,10},{10,1... | collective-permute-start | bytes 6291464 | tf_op jit(solution)/shard_map/ppermute | solution.py:22
  162.1 17.9 %collective-permute-start.7 = (bf16[64,64,256]{2,1,0:T(8,128)(2,1)S(1)}, bf16[64,64,256]{2,1,0:T(8,128)(2,1)S(1)}, u32[]{:S(2)}, u32[]{:S(2)}) collective-permute-start(bf16[64,64,256]{2,1,0:T(8,128)(2,1)S(1)} %pad_maximum_fusion.1), channel_id=1, source_target_pairs={{1,0},{2,1},{3,2},{4,3},{5,4},{6,5},{7,6},{8,7},{9,8},{10,9},{11,1... | collective-permute-start | bytes 6291464 | tf_op jit(solution)/shard_map/ppermute | solution.py:23
  215.2 73.9 %copy-start.4 = (f32[2,32,64,64]{3,2,1,0:T(8,128)S(1)}, f32[2,32,64,64]{3,2,1,0:T(8,128)}, u32[]{:S(2)}) copy-start(f32[2,32,64,64]{3,2,1,0:T(8,128)} %param.17) | copy-start | bytes 3145732
  215.2 46.2 %all-to-all-start = ((f32[64,1,2048]{2,1,0:T(1,128)}), f32[64,1,2048]{2,1,0:T(1,128)S(1)}, u32[]{:S(2)}, u32[]{:S(2)}) async-start(f32[64,1,2048]{2,1,0:T(1,128)} %reshape.218), calls=%async_computation | async-start | bytes 1048576 | tf_op jit(solution)/shard_map/all_to_all | solution.py:187
  267.4 30.2 %copy-start.7 = (f32[64]{0:T(128)S(1)}, f32[64]{0:T(128)}, u32[]{:S(2)}) copy-start(f32[64]{0:T(128)} %param.19) | copy-start | bytes 772
  290.9 7.5 %copy-start.1 = (f32[64,8192]{0,1:T(8,128)S(1)}, f32[64,8192]{0,1:T(8,128)}, u32[]{:S(2)}) copy-start(f32[64,8192]{0,1:T(8,128)} %copy.80) | copy-start | bytes 6291460
